TPU v7x, 512 devices: a whole 4x8x8 slice. The times are simulated.
512 devices in a mesh: row: 16 (over x_lo, z), col: 32 (over x_hi, y, core).
Axes of the slice: x: 4 (x_hi: 2, x_lo: 2; x = x_hi * 2 + x_lo), y: 8, z: 8, core: 2. Of those that a mesh axis runs over, the one named last changes fastest.
Arguments:
- queries: bfloat16 [16, 1024, 512], P('row', 'col'), may hold values from -6 to 6
- keys: bfloat16 [32, 512, 512], P('col', 'row'), may hold values from -6 to 6
- values: bfloat16 [32, 512, 512], P('col', 'row'), may hold values from -6 to 6
- outputs: bfloat16 [16, 1024, 512], P('row', 'col'), may hold values from -2 to 2
- grad_out: bfloat16 [16, 1024, 512], P('row', 'col'), may hold values from -48 to 48
- lse: float32 [16, 8, 1024], P('row'), may hold values from 7 to 9.5
- tile_slot: int32 [16, 32, 24], P('row', 'col'), may hold values from 0 to 31, as said below
- tile_live: int32 [16, 32], P('row', 'col'), may hold values from 1 to 24, as said below
- tile_bits: int32 [16, 32, 24, 8, 128], P('row', 'col'), may hold values from 0 to 65535, as said below
Outputs:
- grad_queries: bfloat16 [16, 1024, 512], P('row', 'col')
- grad_keys: bfloat16 [32, 512, 512], P('col', 'row')
- grad_values: bfloat16 [32, 512, 512], P('col', 'row')
Inputs may be any that keep to these rules, and one draw needn't show every extreme that they name: `tile_slot`: the 24 entries of one pair of blocks are distinct slots. `tile_live`: some pair of blocks has all 24 entries live. `tile_bits`: each word holds 16 edge bits in its low bits.
All inputs are finite; a program needn't handle non-finite values.
Results may differ from a plain program's by a relative error of at most 0.02.
Values may be sent and summed in bfloat16 or wider, within the bound.
A program may use at most 64 MiB of HBM per device.

v0:
```python
import jax
import jax.numpy as jnp
from jax import lax
from jax.sharding import PartitionSpec as P


def unpack_bits(packed_rows):
    shifts = jnp.arange(16, dtype=jnp.int32)
    bit_values = jnp.bitwise_and(jnp.right_shift(packed_rows[:, :, None], shifts), 1)
    return (
        jnp.transpose(bit_values, (1, 0, 2)).reshape(
            packed_rows.shape[1], packed_rows.shape[0] * 16
        )
        == 1
    )


def row_delta(grads, outs, head_count):
    leading = grads.shape[:-1]
    model_width = grads.shape[-1]
    product = (grads.astype(jnp.float32) * outs.astype(jnp.float32)).reshape(
        leading + (head_count, model_width // head_count)
    )
    return jnp.swapaxes(jnp.sum(product, axis=-1), -1, -2).astype(jnp.bfloat16)


def add_rows(total, piece, start):
    current = lax.dynamic_slice_in_dim(total, start, piece.shape[0], 0)
    return lax.dynamic_update_slice_in_dim(total, current + piece, start, 0)


def body(queries, keys, values, outputs, grad_out, lse, tile_slot, tile_live, tile_bits):
    head_count = lse.shape[1]
    model_width = queries.shape[2]
    head_dim = model_width // head_count
    tile_size = tile_bits.shape[4]
    scaling = float(head_dim) ** (-0.5)
    query_all, grad_all, out_all = (
        lax.all_gather(queries, "col", axis=1, tiled=True),
        lax.all_gather(grad_out, "col", axis=1, tiled=True),
        lax.all_gather(outputs, "col", axis=1, tiled=True),
    )
    delta_rows = row_delta(grad_all, out_all, head_count)[0]
    key_all, value_all = (
        lax.all_gather(keys, "row", axis=1, tiled=True),
        lax.all_gather(values, "row", axis=1, tiled=True),
    )
    query_block = query_all[0]
    grad_block = grad_all[0]
    key_block = key_all[0]
    value_block = value_all[0]
    lse_rows = lse[0]
    slot_list = tile_slot[0, 0]
    live_count = tile_live[0, 0]
    packed = tile_bits[0, 0]
    key_tiles = key_block.shape[0] // tile_size

    def starts_of(slot_index):
        slot_value = slot_list[slot_index]
        return (slot_value // key_tiles * tile_size, slot_value % key_tiles * tile_size)

    def key_tile_of(k_start):
        return lax.dynamic_slice_in_dim(key_block, k_start, tile_size, 0).reshape(
            tile_size, head_count, head_dim
        )

    def tile_core(slot_index):
        q_start, k_start = starts_of(slot_index)
        q_tile = lax.dynamic_slice_in_dim(query_block, q_start, tile_size, 0).reshape(
            tile_size, head_count, head_dim
        )
        g_tile = lax.dynamic_slice_in_dim(grad_block, q_start, tile_size, 0).reshape(
            tile_size, head_count, head_dim
        )
        k_tile = key_tile_of(k_start)
        v_tile = lax.dynamic_slice_in_dim(value_block, k_start, tile_size, 0).reshape(
            tile_size, head_count, head_dim
        )
        lse_tile = lax.dynamic_slice_in_dim(lse_rows, q_start, tile_size, 1)
        delta_tile = lax.dynamic_slice_in_dim(delta_rows, q_start, tile_size, 1).astype(jnp.float32)
        edge_mask = jnp.logical_and(unpack_bits(packed[slot_index]), slot_index < live_count)
        scores = (
            jnp.einsum("ihd,jhd->hij", q_tile, k_tile, preferred_element_type=jnp.float32) * scaling
        )
        attn_prob = jnp.where(edge_mask[None], jnp.exp(scores - lse_tile[:, :, None]), 0.0)
        prob_low = attn_prob.astype(jnp.bfloat16)
        value_tile_grad = jnp.einsum(
            "hij,ihd->jhd", prob_low, g_tile, preferred_element_type=jnp.float32
        ).reshape(tile_size, model_width)
        grad_prob = jnp.einsum("ihd,jhd->hij", g_tile, v_tile, preferred_element_type=jnp.float32)
        score_low = (attn_prob * (grad_prob - delta_tile[:, :, None])).astype(jnp.bfloat16)
        key_tile_grad = (
            jnp.einsum(
                "hij,ihd->jhd", score_low, q_tile, preferred_element_type=jnp.float32
            ).reshape(tile_size, model_width)
            * scaling
        )
        return (q_start, k_start, k_tile, score_low, key_tile_grad, value_tile_grad)

    def query_piece(score_low, k_tile):
        return (
            jnp.einsum(
                "hij,jhd->ihd", score_low, k_tile, preferred_element_type=jnp.float32
            ).reshape(tile_size, model_width)
            * scaling
        )

    limit = packed.shape[0]
    key_zeros = jnp.zeros(key_block.shape, jnp.float32)

    def one_tile(slot_index, running):
        grad_q, grad_k, grad_v = running
        q_start, k_start, k_tile, score_low, key_tile_grad, value_tile_grad = tile_core(slot_index)
        grad_q = add_rows(grad_q, query_piece(score_low, k_tile), q_start)
        grad_k = add_rows(grad_k, key_tile_grad, k_start)
        grad_v = add_rows(grad_v, value_tile_grad, k_start)
        return (grad_q, grad_k, grad_v)

    start_sums = (jnp.zeros(query_block.shape, jnp.float32), key_zeros, key_zeros)
    grad_q, grad_k, grad_v = lax.fori_loop(0, limit, one_tile, start_sums)
    query_grad_sum = lax.psum_scatter(
        grad_q[None].astype(jnp.bfloat16), "col", scatter_dimension=1, tiled=True
    )
    key_grad_sum, value_grad_sum = (
        lax.psum_scatter(
            grad_k[None].astype(jnp.bfloat16), "row", scatter_dimension=1, tiled=True
        ).astype(jnp.float32),
        lax.psum_scatter(
            grad_v[None].astype(jnp.bfloat16), "row", scatter_dimension=1, tiled=True
        ).astype(jnp.float32),
    )
    return (query_grad_sum, key_grad_sum.astype(jnp.bfloat16), value_grad_sum.astype(jnp.bfloat16))


def solution(mesh):
    in_specs = (
        P("row", "col", None),
        P("col", "row", None),
        P("col", "row", None),
        P("row", "col", None),
        P("row", "col", None),
        P("row", None, None),
        P("row", "col", None),
        P("row", "col"),
        P("row", "col", None, None, None),
    )
    out_specs = (P("row", "col", None), P("col", "row", None), P("col", "row", None))
    return jax.shard_map(body, mesh=mesh, in_specs=in_specs, out_specs=out_specs, check_vma=False)
```

profile of v0, /device:TPU:1, one launch (start us, length us, event | category | flops | bytes accessed | tf_op | source)
XLA Modules:
  0.0 910.8 jit_solution(6940558741833403063)
XLA Ops:
  9.4 38.5 %all_gather.15 = bf16[1,512,512]{2,1,0:T(8,128)(2,1)} all-gather(bf16[1,32,512]{2,1,0:T(8,128)(2,1)} %param.12), channel_id=1, replica_groups=mesh['row'=16,'col'=32] {'row'}, dimensions={1}, use_global_device_ids=true | all-gather | bytes 557056 | tf_op jit(solution)/shard_map/all_gather | solution.py:45
  47.9 29.0 %all_gather.18 = bf16[1,512,512]{2,1,0:T(8,128)(2,1)} all-gather(bf16[1,32,512]{2,1,0:T(8,128)(2,1)} %param.13), channel_id=1, replica_groups=mesh['row'=16,'col'=32] {'row'}, dimensions={1}, use_global_device_ids=true | all-gather | bytes 557056 | tf_op jit(solution)/shard_map/all_gather | solution.py:46
  76.9 23.9 %all-gather.8.cloned.1.call-done = bf16[1,1024,512]{2,1,0:T(8,128)(2,1)} async-done(((bf16[1,32,512]{2,1,0:T(8,128)(2,1)}), bf16[1,1024,512]{2,1,0:T(8,128)(2,1)}) %all-gather.8.cloned.1.call-update) | async-done | bytes 1048592 | tf_op jit(solution)/shard_map/all_gather | solution.py:41
  100.8 1.5 copy.40
  102.3 81.2 %all-gather.6.cloned.1.call-done = bf16[1,1024,512]{2,1,0:T(8,128)(2,1)} async-done(((bf16[1,32,512]{2,1,0:T(8,128)(2,1)}), bf16[1,1024,512]{2,1,0:T(8,128)(2,1)}) %all-gather.6.cloned.1.call-update) | async-done | bytes 1048592 | tf_op jit(solution)/shard_map/all_gather | solution.py:40
  183.5 2.3 copy.39
  185.7 1.6 convert_multiply_fusion
  187.6 79.2 %all-gather.4.cloned.1.call-done = bf16[1,1024,512]{2,1,0:T(8,128)(2,1)} async-done(((bf16[1,32,512]{2,1,0:T(8,128)(2,1)}), bf16[1,1024,512]{2,1,0:T(8,128)(2,1)}) %all-gather.4.cloned.1.call-update) | async-done | bytes 1048592 | tf_op jit(solution)/shard_map/all_gather | solution.py:39
  266.9 1.1 broadcast_in_dim.55.clone
  268.0 1.6 broadcast_in_dim.54.clone
  269.6 371.2 %while.19 = (s32[]{:T(128)}, f32[1024,512]{1,0:T(8,128)}, f32[512,512]{1,0:T(8,128)}, f32[512,512]{1,0:T(8,128)S(1)}, s32[24]{0:T(128)S(1)}, /*index=5*/bf16[512...) while((s32[]{:T(128)}, f32[1024,512]{1,0:T(8,128)}, ...), condition=%wide.region_2.3_spmd, body=%wide.region_1.2_spmd.sunk | while | flops 85197856 | bytes 14914090 | solution.py:120
  279.4 1.0 constant_dynamic-slice_fusion.17
  325.7 1.0 constant_dynamic-slice_fusion.17
  356.7 1.0 constant_dynamic-slice_fusion.17
  373.2 1.0 constant_dynamic-slice_fusion.24
  388.7 1.0 constant_dynamic-slice_fusion.24
  404.2 1.0 constant_dynamic-slice_fusion.24
  418.5 1.0 constant_dynamic-slice_fusion.17
  450.6 1.0 constant_dynamic-slice_fusion.24
  641.8 2.1 convert_bitcast_fusion.2
  643.9 2.7 convert_bitcast_fusion
  646.7 54.3 %reduce-scatter.8.cloned.1.call-done = bf16[1,32,512]{2,1,0:T(8,128)(2,1)} async-done(((bf16[1,512,512]{2,1,0:T(8,128)(2,1)}), bf16[1,32,512]{2,1,0:T(8,128)(2,1)}) %reduce-scatter.8.cloned.1.call-update) | async-done | bytes 32784 | tf_op jit(solution)/shard_map/reduce_scatter | solution.py:128
  700.9 73.0 %reduce-scatter.6.cloned.1.call-done = bf16[1,32,512]{2,1,0:T(8,128)(2,1)} async-done(((bf16[1,512,512]{2,1,0:T(8,128)(2,1)}), bf16[1,32,512]{2,1,0:T(8,128)(2,1)}) %reduce-scatter.6.cloned.1.call-update) | async-done | bytes 32784 | tf_op jit(solution)/shard_map/reduce_scatter | solution.py:125
  774.0 130.0 %reduce-scatter.4.cloned.1.call-done = bf16[1,32,512]{2,1,0:T(8,128)(2,1)} async-done(((bf16[1,1024,512]{2,1,0:T(8,128)(2,1)}), bf16[1,32,512]{2,1,0:T(8,128)(2,1)}) %reduce-scatter.4.cloned.1.call-update) | async-done | bytes 32784 | tf_op jit(solution)/shard_map/reduce_scatter | solution.py:121
  (849 shorter events, 284.7 us)
Async XLA Ops:
  7.2 93.6 %all-gather.8.cloned.1.call-start = ((), (), s32[]{:S(2)}) async-start(), calls=%async_computation.5 | async-start | bytes 1081344 | tf_op jit(solution)/shard_map/all_gather | solution.py:41
  7.9 175.6 %all-gather.6.cloned.1.call-start = ((), (), s32[]{:S(2)}) async-start(), calls=%async_computation.4 | async-start | bytes 1081344 | tf_op jit(solution)/shard_map/all_gather | solution.py:40
  8.6 258.1 %all-gather.4.cloned.1.call-start = ((), (), s32[]{:S(2)}) async-start(), calls=%async_computation.3 | async-start | bytes 1081344 | tf_op jit(solution)/shard_map/all_gather | solution.py:39
  9.4 691.6 %reduce-scatter.8.cloned.1.call-start = ((), (), s32[]{:S(2)}) async-start(), calls=%async_computation.8 | async-start | bytes 557056 | tf_op jit(solution)/shard_map/reduce_scatter | solution.py:128
  266.8 2.8 copy-start
  641.7 132.2 %reduce-scatter.6.cloned.1.call-start = ((), (), s32[]{:S(2)}) async-start(), calls=%async_computation.7 | async-start | bytes 557056 | tf_op jit(solution)/shard_map/reduce_scatter | solution.py:125
  643.9 260.1 %reduce-scatter.4.cloned.1.call-start = ((), (), s32[]{:S(2)}) async-start(), calls=%async_computation.6 | async-start | bytes 1081344 | tf_op jit(solution)/shard_map/reduce_scatter | solution.py:121
Sparse Core Ops, SparseCore 0:
  11.4 89.3 all-gather.7
  104.1 79.2 all-gather.5
  186.8 79.9 all-gather.3
  641.9 59.0 reduce-scatter.7
  704.4 69.5 reduce-scatter.5
  779.0 124.9 reduce-scatter.3
where the time goes:
time: 921 us; the launch traced here: 911 us
  waiting for transfers between devices  444 us (48%)
  local copies, waits for them, and re-layouts  259 us (28%)
  loops' own time  82.3 us (9%)
  blocking collectives  67.5 us (7%)
  matrix products  32 us (3%)
  between operations  14.1 us (2%)
  other arithmetic  12.2 us (1%)
    reduce_scatter x1, waiting for transfers between devices, body(): lax.psum_scatter(grad_q[None].astype(jnp.bfloat16), 'col', scatter_dimens...  130 us
    another operation x1, loops' own time, body(): grad_q, grad_k, grad_v = lax.fori_loop(0, limit, one_tile, start_sums)  82.3 us
    all_gather x1, waiting for transfers between devices, body(): lax.all_gather(grad_out, 'col', axis=1, tiled=True)  81.2 us
    all_gather x1, waiting for transfers between devices, body(): lax.all_gather(queries, 'col', axis=1, tiled=True)  79.2 us
    reduce_scatter x1, waiting for transfers between devices, body(): lax.psum_scatter(grad_k[None].astype(jnp.bfloat16), 'row', scatter_dimens...  73 us
    dynamic_slice x144, local copies, waits for them, and re-layouts, add_rows(): current = lax.dynamic_slice_in_dim(total, start, piece.shape[0], 0)  56.2 us
    reduce_scatter x1, waiting for transfers between devices, body(): lax.psum_scatter(grad_v[None].astype(jnp.bfloat16), 'row', scatter_dimens...  54.3 us
    dynamic_update_slice x120, local copies, waits for them, and re-layouts, add_rows(): return lax.dynamic_update_slice_in_dim(total, current + piece, start, 0)  44.4 us
  transfers between devices with their start and end apart: 6, of which 6 were waited for; matrix products, arithmetic and copies ran while one was open for 1% of the time, Pallas kernels for 0%

commit v1 on v0

v1 whole, which is shorter than its diff:
```python
import functools
import math

import jax
import jax.numpy as jnp
from jax import lax
from jax.experimental import pallas as pl
from jax.experimental.pallas import tpu as pltpu
from jax.sharding import PartitionSpec as P

MESH = pl.DeviceIdType.MESH
RING = 8
PIECE = 32
NEG = -1e30
F32 = jnp.float32
BF16 = jnp.bfloat16


def places():
    r, col = lax.axis_index("row"), lax.axis_index("col")
    xl, z = r // RING, lax.rem(r, RING)
    c = lax.rem(col, 2)
    y = lax.rem(col // 2, RING)
    xh = col // (2 * RING)
    return xl, z, xh, y, c


def turn(a, d):
    return lax.rem(a + d + RING, RING)


def q_rows(xh, y, c):
    return pl.ds(pl.multiple_of((xh * 16 + y * 2 + c) * PIECE, PIECE), PIECE)


def k_rows(xl, z):
    return pl.ds(pl.multiple_of((xl * 8 + z) * PIECE, PIECE), PIECE)


def neighbours(xl, z, xh, y, c):
    def on_col(xh, y, c):
        return {"col": xh * 16 + y * 2 + c}

    def on_row(xl, z):
        return {"row": xl * 8 + z}

    return {
        "qx": on_col(1 - xh, y, c),
        "qc": on_col(xh, y, 1 - c),
        "q+": on_col(xh, turn(y, 1), c),
        "q-": on_col(xh, turn(y, -1), c),
        "kx": on_row(1 - xl, z),
        "k+": on_row(xl, turn(z, 1)),
        "k-": on_row(xl, turn(z, -1)),
    }


def greet(near):
    barrier = pltpu.get_barrier_semaphore()
    for where in near.values():
        pl.semaphore_signal(barrier, inc=1, device_id=where, device_id_type=MESH)
    pl.semaphore_wait(barrier, len(near))


class Post:
    def __init__(self, send, recv):
        self.send, self.recv, self.count, self.sent = send, recv, 0, []

    def slot(self):
        self.count += 1
        return self.count - 1

    def put(self, slot, src, dst, where):
        copy = pltpu.make_async_remote_copy(
            src_ref=src,
            dst_ref=dst,
            send_sem=self.send.at[slot],
            recv_sem=self.recv.at[slot],
            device_id=where,
            device_id_type=MESH,
        )
        copy.start()
        self.sent.append(copy)

    def got(self, slot, dst):
        pltpu.make_async_copy(dst, dst, self.recv.at[slot]).wait()

    def finish(self):
        for copy in self.sent:
            copy.wait_send()


def gather_kernel(q, g, o, k, v, qa, ga, ka, va, own_g, own_sem, send, recv):
    xl, z, xh, y, c = places()
    near = neighbours(xl, z, xh, y, c)
    greet(near)
    post = Post(send, recv)

    def spread(kind, own, full, rows_of, here, reach):
        pos, ring = here
        slots = {}
        for s in ("own", "mate"):
            for sign, far in reach:
                for d in range(1, far + 1):
                    slots[s, sign, d] = post.slot()
        slots["mate"] = post.slot()
        return dict(kind=kind, own=own, full=full, rows=rows_of, pos=pos, ring=ring, reach=reach, slots=slots)

    long_plus = ((1, 4), (-1, 3))
    long_minus = ((1, 3), (-1, 4))
    q_of = lambda x, t, core: q_rows(x, t, core)
    k_of = lambda x, t, core: k_rows(x, t)
    streams = [
        spread("k", k, ka, k_of, (xl, z), long_plus),
        spread("q", q, qa, q_of, (xh, y), long_plus),
        spread("k", v, va, k_of, (xl, z), long_minus),
        spread("q", own_g, ga, q_of, (xh, y), long_minus),
    ]
    for st in streams:
        if st["kind"] == "q":
            st["core"] = {}
            for s in ("own", "mate"):
                st["core"][s, 0] = post.slot()
                for sign, far in st["reach"]:
                    for d in range(1, far + 1):
                        st["core"][s, sign * d] = post.slot()

    def part_of(st, s):
        return st["pos"] if s == "own" else 1 - st["pos"]

    def ring_send(st, s, sign, d, src):
        rows = st["rows"](part_of(st, s), turn(st["ring"], -sign * (d - 1)), c)
        if src is None:
            src = st["full"].at[rows]
        way = st["kind"] + ("+" if sign > 0 else "-")
        post.put(st["slots"][s, sign, d], src, st["full"].at[rows], near[way])

    def core_send(st, s, shift, src):
        if st["kind"] != "q":
            return
        rows = st["rows"](part_of(st, s), turn(st["ring"], -shift), c)
        if src is None:
            src = st["full"].at[rows]
        post.put(st["core"][s, shift], src, st["full"].at[rows], near["qc"])

    def begin(st):
        rows = st["rows"](st["pos"], st["ring"], c)
        post.put(st["slots"]["mate"], st["own"], st["full"].at[rows], near[st["kind"] + "x"])
        for sign, far in st["reach"]:
            ring_send(st, "own", sign, 1, st["own"])
        core_send(st, "own", 0, st["own"])

    for st in streams[:3]:
        begin(st)

    product = g[...].astype(F32) * o[...].astype(F32)
    lane = lax.broadcasted_iota(jnp.int32, (PIECE, 128), 1)
    delta = jnp.zeros((PIECE, 128), F32)
    for h in range(8):
        one = jnp.sum(product[:, h * 64 : (h + 1) * 64], axis=1, keepdims=True)
        delta = jnp.where(lane == h, one, delta)
    own_g[:, 0:512] = g[...]
    own_g[:, 512:640] = delta.astype(BF16)
    begin(streams[3])

    keep = []
    for n, st in enumerate(streams):
        rows = st["rows"](st["pos"], st["ring"], c)
        copy = pltpu.make_async_copy(st["own"], st["full"].at[rows], own_sem.at[n])
        copy.start()
        keep.append(copy)

    for st in streams:
        rows = st["rows"](1 - st["pos"], st["ring"], c)
        post.got(st["slots"]["mate"], st["full"].at[rows])
        for sign, far in st["reach"]:
            ring_send(st, "mate", sign, 1, None)
        core_send(st, "mate", 0, None)

    for d in range(1, 5):
        for s in ("own", "mate"):
            for st in streams:
                for sign, far in st["reach"]:
                    if d > far:
                        continue
                    rows = st["rows"](part_of(st, s), turn(st["ring"], -sign * d), c)
                    post.got(st["slots"][s, sign, d], st["full"].at[rows])
                    if d < far:
                        ring_send(st, s, sign, d + 1, None)
                    core_send(st, s, sign * d, None)

    for st in streams:
        if st["kind"] == "q":
            for (s, shift), slot in st["core"].items():
                rows = st["rows"](part_of(st, s), turn(st["ring"], -shift), 1 - c)
                post.got(slot, st["full"].at[rows])
    for copy in keep:
        copy.wait()
    post.finish()


GATHER_COPIES = 2 * 15 + 2 * (15 + 16)


def gather(q, g, o, k, v):
    shapes = [(1024, 512), (1024, 640), (512, 512), (512, 512)]
    return pl.pallas_call(
        gather_kernel,
        out_shape=[jax.ShapeDtypeStruct(s, BF16) for s in shapes],
        in_specs=[pl.BlockSpec(memory_space=pltpu.VMEM)] * 5,
        out_specs=[pl.BlockSpec(memory_space=pltpu.VMEM)] * 4,
        scratch_shapes=[
            pltpu.VMEM((PIECE, 640), BF16),
            pltpu.SemaphoreType.DMA((4,)),
            pltpu.SemaphoreType.DMA((GATHER_COPIES,)),
            pltpu.SemaphoreType.DMA((GATHER_COPIES,)),
        ],
        compiler_params=pltpu.CompilerParams(collective_id=0, has_side_effects=True),
        name="gather",
    )(q, g, o, k, v)


def scatter_kernel(dq, dk, dv, oq, ok, ov, mine, land, core_land, mate_out, mate_land, send, recv):
    xl, z, xh, y, c = places()
    near = neighbours(xl, z, xh, y, c)
    greet(near)
    post = Post(send, recv)

    order = [4, -4 + 1, 3, -2, 2, -1, 1, 0]
    core_slots = {}
    for n, shift in enumerate(order):
        t = turn(y, shift)
        for a in range(2):
            slot = post.slot()
            core_slots[a, shift] = (slot, n * 2 + a)
            post.put(slot, dq.at[q_rows(a, t, 1 - c)], core_land.at[n * 2 + a], near["qc"])

    def q_part(a, shift):
        slot, n = core_slots[a, shift]
        if shift is not None and (a, shift) not in q_part.seen:
            post.got(slot, core_land.at[n])
            q_part.seen.add((a, shift))
        return dq[q_rows(a, turn(y, shift), c), :].astype(F32) + core_land[n].astype(F32)

    q_part.seen = set()

    def k_part(ref):
        return lambda a, shift: ref[k_rows(a, turn(z, shift)), :].astype(F32)

    chains = []
    count = 0
    for a in range(2):
        for kind, part, reach, ref in (
            ("k", k_part(dk), ((1, 4), (-1, 3)), dk),
            ("k", k_part(dv), ((1, 3), (-1, 4)), dv),
            ("q", q_part, ((1, 4), (-1, 3)) if a == 0 else ((1, 3), (-1, 4)), None),
        ):
            for sign, far in reach:
                chains.append(dict(a=a, kind=kind, part=part, sign=sign, far=far, ref=ref, base=count))
                count += far
    for ch in chains:
        ch["slots"] = [post.slot() for _ in range(ch["far"])]

    for s in range(4):
        for ch in chains:
            far, sign, a = ch["far"], ch["sign"], ch["a"]
            if s >= far:
                continue
            shift = sign * (far - s)
            if shift == -4:
                shift = 4
            here = ch["base"] + s
            way = near[ch["kind"] + ("+" if sign > 0 else "-")]
            if s == 0 and ch["ref"] is not None:
                src = ch["ref"].at[k_rows(a, turn(z, shift))]
            else:
                total = ch["part"](a, shift)
                if s > 0:
                    post.got(ch["slots"][s - 1], land.at[here - 1])
                    total = total + land[here - 1].astype(F32)
                mine[here] = total.astype(BF16)
                src = mine.at[here]
            post.put(ch["slots"][s], src, land.at[here], way)

    mates = [post.slot() for _ in range(3)]
    finals = []
    for n, (kind, pos) in enumerate((("k", xl), ("k", xl), ("q", xh))):
        both = []
        for a in range(2):
            pair = [ch for ch in chains if ch["a"] == a][2 * n : 2 * n + 2]
            total = pair[0]["part"](a, 0)
            for ch in pair:
                last = ch["base"] + ch["far"] - 1
                post.got(ch["slots"][-1], land.at[last])
                total = total + land[last].astype(F32)
            both.append(total)
        here_first = pos == 0
        mate_out[n] = jnp.where(here_first, both[1], both[0]).astype(BF16)
        post.put(mates[n], mate_out.at[n], mate_land.at[n], near[kind + "x"])
        finals.append(jnp.where(here_first, both[0], both[1]))
    for n, out in enumerate((ok, ov, oq)):
        post.got(mates[n], mate_land.at[n])
        out[...] = (finals[n] + mate_land[n].astype(F32)).astype(BF16)
    post.finish()


SCATTER_COPIES = 16 + 42 + 3


def scatter(dq, dk, dv):
    return pl.pallas_call(
        scatter_kernel,
        out_shape=[jax.ShapeDtypeStruct((PIECE, 512), BF16)] * 3,
        in_specs=[pl.BlockSpec(memory_space=pltpu.VMEM)] * 3,
        out_specs=[pl.BlockSpec(memory_space=pltpu.VMEM)] * 3,
        scratch_shapes=[
            pltpu.VMEM((42, PIECE, 512), BF16),
            pltpu.VMEM((42, PIECE, 512), BF16),
            pltpu.VMEM((16, PIECE, 512), BF16),
            pltpu.VMEM((3, PIECE, 512), BF16),
            pltpu.VMEM((3, PIECE, 512), BF16),
            pltpu.SemaphoreType.DMA((SCATTER_COPIES,)),
            pltpu.SemaphoreType.DMA((SCATTER_COPIES,)),
        ],
        compiler_params=pltpu.CompilerParams(collective_id=1, has_side_effects=True),
        name="scatter",
    )(dq, dk, dv)


def attention_kernel(slots, live, q, g, k, v, lse, bits, dq, dk, dv, bias, delta_t, qt, gt, kc, vc, kt, prob, score):
    rows, keys = q.shape[0], k.shape[0]
    scale = 0.125
    bias[...] = jnp.full(bias.shape, NEG, F32)
    bit_of = lax.broadcasted_iota(jnp.int32, (16, 128), 0)

    @pl.loop(0, live[0, 0])
    def _(e):
        slot = slots[0, 0, e]
        across = pl.multiple_of((slot // 4) * 128, 128)
        down = pl.multiple_of(lax.rem(slot, 4) * 128, 128)
        words = bits[e]
        for r in range(8):
            word = jnp.broadcast_to(words[r : r + 1, :], (16, 128))
            edge = jnp.bitwise_and(jnp.right_shift(word, bit_of), 1)
            bias[pl.ds(down + r * 16, 16), pl.ds(across, 128)] = jnp.where(edge == 1, 0.0, NEG)

    delta_t[...] = g[:, 512:640].astype(F32).T

    @pl.loop(0, 4)
    def _(p):
        lanes = pl.ds(pl.multiple_of(p * 128, 128), 128)
        kp = k[:, lanes].astype(F32)
        vp = v[:, lanes].astype(F32)
        qp_t = q[:, lanes].T
        gp_t = g[:, lanes].T
        kt[...] = k[:, lanes].T
        lane = lax.broadcasted_iota(jnp.int32, (keys, 128), 1)
        row = lax.broadcasted_iota(jnp.int32, (16, rows), 0)
        for a in range(2):
            own = (lane < 64) if a == 0 else (lane >= 64)
            free = 64 * (1 - a)
            kc[a] = jnp.where(own, kp, jnp.where(lane < free + 3, 1.0, 0.0) if a == 1 else jnp.where(lane < 67, 1.0, 0.0)).astype(BF16)
            vc[a] = jnp.where(own, vp, jnp.where(lane < free + 1, 1.0, 0.0)).astype(BF16)
            low = lse[pl.ds(2 * p + a, 1), :] * (-8.0)
            first = low.astype(BF16).astype(F32)
            second = (low - first).astype(BF16).astype(F32)
            third = low - first - second
            qt[a] = qp_t
            qt[a, free : free + 16, :] = jnp.where(
                row == 0, first, jnp.where(row == 1, second, jnp.where(row == 2, third, 0.0))
            ).astype(BF16)
            gt[a] = gp_t
            gt[a, free : free + 16, :] = jnp.where(
                row == 0, -delta_t[pl.ds(2 * p + a, 1), :], 0.0
            ).astype(BF16)
        parts = []
        for a in range(2):
            for ib in range(rows // 256):
                for jb in range(keys // 128):
                    js, is_ = slice(jb * 128, jb * 128 + 128), slice(ib * 256, ib * 256 + 256)
                    s = jnp.dot(kc[a, js, :], qt[a, :, is_], preferred_element_type=F32)
                    w = jnp.dot(vc[a, js, :], gt[a, :, is_], preferred_element_type=F32)
                    pr = jnp.exp2(s * (scale * math.log2(math.e)) + bias[js, is_])
                    prob[js, is_] = pr.astype(BF16)
                    score[js, is_] = (pr * w).astype(BF16)
            value_sum = jnp.dot(prob[...], g[:, lanes], preferred_element_type=F32)
            key_sum = jnp.dot(score[...], q[:, lanes], preferred_element_type=F32)
            query_sum = jnp.dot(kt[64 * a : 64 * a + 64, :], score[...], preferred_element_type=F32)
            parts.append((value_sum, key_sum, query_sum))
        dv[:, lanes] = jnp.where(lane < 64, parts[0][0], parts[1][0]).astype(BF16)
        dk[:, lanes] = (jnp.where(lane < 64, parts[0][1], parts[1][1]) * scale).astype(BF16)
        both = jnp.concatenate([parts[0][2], parts[1][2]], axis=0) * scale
        dq[:, lanes] = both.T.astype(BF16)


def attention(slots, live, q, g, k, v, lse, bits):
    rows, keys = q.shape[0], k.shape[0]
    vmem = pl.BlockSpec(memory_space=pltpu.VMEM)
    smem = pl.BlockSpec(memory_space=pltpu.SMEM)
    return pl.pallas_call(
        attention_kernel,
        out_shape=[jax.ShapeDtypeStruct((n, 512), BF16) for n in (rows, keys, keys)],
        in_specs=[smem] * 2 + [vmem] * 6,
        out_specs=[vmem] * 3,
        scratch_shapes=[
            pltpu.VMEM((keys, rows), F32),
            pltpu.VMEM((128, rows), F32),
            pltpu.VMEM((2, 128, rows), BF16),
            pltpu.VMEM((2, 128, rows), BF16),
            pltpu.VMEM((2, keys, 128), BF16),
            pltpu.VMEM((2, keys, 128), BF16),
            pltpu.VMEM((128, keys), BF16),
            pltpu.VMEM((keys, rows), BF16),
            pltpu.VMEM((keys, rows), BF16),
        ],
        compiler_params=pltpu.CompilerParams(vmem_limit_bytes=48 << 20),
        name="attention",
    )(slots, live, q, g, k, v, lse, bits)


def body(queries, keys, values, outputs, grad_out, lse, tile_slot, tile_live, tile_bits):
    q, g, k, v = gather(queries[0], grad_out[0], outputs[0], keys[0], values[0])
    dq, dk, dv = attention(tile_slot, tile_live, q, g, k, v, lse[0], tile_bits[0, 0])
    oq, ok, ov = scatter(dq, dk, dv)
    return oq[None], ok[None], ov[None]


def solution(mesh):
    in_specs = (
        P("row", "col", None),
        P("col", "row", None),
        P("col", "row", None),
        P("row", "col", None),
        P("row", "col", None),
        P("row", None, None),
        P("row", "col", None),
        P("row", "col"),
        P("row", "col", None, None, None),
    )
    out_specs = (P("row", "col", None), P("col", "row", None), P("col", "row", None))
    return jax.shard_map(body, mesh=mesh, in_specs=in_specs, out_specs=out_specs, check_vma=False)
```

time: 921 us -> 90.5 us (0.10)
  the two profiles are of different devices: /device:TPU:1 before, /device:TPU:16 now
where the time goes in v1:
time: 90.5 us; the launch traced here: 89.8 us
  Pallas kernels  74.9 us (83%)
  local copies, waits for them, and re-layouts  13.6 us (15%)
  between operations  1.33 us (1%)
    pallas_call x1, Pallas kernels, gather(): pl.pallas_call(gather_kernel, out_shape=[jax.ShapeDtypeStruct(s, BF16) fo...  36.4 us
    pallas_call x1, Pallas kernels, scatter(): pl.pallas_call(scatter_kernel, out_shape=[jax.ShapeDtypeStruct((PIECE, 51...  26.3 us
    unnamed x23, local copies, waits for them, and re-layouts  13.6 us
    pallas_call x1, Pallas kernels, attention(): pl.pallas_call(attention_kernel, out_shape=[jax.ShapeDtypeStruct((n, 512)...  12.1 us

profile of v1, /device:TPU:16, one launch (start us, length us, event | category | flops | bytes accessed | tf_op | source)
XLA Modules:
  0.0 89.8 jit_solution(1111931185392749639)
XLA Ops:
  1.3 36.4 %gather.1 = (bf16[1024,512]{1,0:T(8,128)(2,1)}, bf16[1024,640]{1,0:T(8,128)(2,1)}, bf16[512,512]{1,0:T(8,128)(2,1)}, bf16[512,512]{1,0:T(8,128)(2,1)}) custom-call(bf16[32,512]{1,0:T(8,128)(2,1)} %bitcast.12, bf16[32,512]{1,0:T(8,128)(2,1)} %bitcast.13, bf16[32,512]{1,0:T(8,128)(2,1)} %bitcast.14, bf16[32,512]{1,0:T(8,128)(2,1)} %bitcast.15, ...), custom_call_target="tpu_custom_call" | custom-call | tf_op jit(solution)/shard_map/gather/pallas_call | solution.py:207
  37.7 0.0 copy-start
  37.7 1.3 %copy-done = bf16[1024,640]{1,0:T(8,128)(2,1)S(1)} copy-done((bf16[1024,640]{1,0:T(8,128)(2,1)S(1)}, bf16[1024,640]{1,0:T(8,128)(2,1)}, u32[]{:S(2)}) %copy-start) | copy-done | bytes 1310744
  39.0 0.0 copy-start.2
  39.0 1.2 %copy-done.2 = bf16[1024,512]{1,0:T(8,128)(2,1)S(1)} copy-done((bf16[1024,512]{1,0:T(8,128)(2,1)S(1)}, bf16[1024,512]{1,0:T(8,128)(2,1)}, u32[]{:S(2)}) %copy-start.2) | copy-done | bytes 1048600
  40.2 0.0 copy-start.5
  40.2 1.0 %copy-done.5 = bf16[512,512]{1,0:T(8,128)(2,1)S(1)} copy-done((bf16[512,512]{1,0:T(8,128)(2,1)S(1)}, bf16[512,512]{1,0:T(8,128)(2,1)}, u32[]{:S(2)}) %copy-start.5) | copy-done | bytes 524312
  41.3 0.0 copy-start.6
  41.3 1.0 %copy-done.6 = bf16[512,512]{1,0:T(8,128)(2,1)S(1)} copy-done((bf16[512,512]{1,0:T(8,128)(2,1)S(1)}, bf16[512,512]{1,0:T(8,128)(2,1)}, u32[]{:S(2)}) %copy-start.6) | copy-done | bytes 524312
  42.3 0.0 copy-start.7
  42.3 0.9 copy-done.7
  43.2 0.0 copy-start.8
  43.2 0.8 copy-done.8
  44.0 0.0 copy-start.9
  44.0 0.7 copy-done.9
  44.6 12.1 %attention.1 = (bf16[1024,512]{1,0:T(8,128)(2,1)S(1)}, bf16[512,512]{1,0:T(8,128)(2,1)S(1)}, bf16[512,512]{1,0:T(8,128)(2,1)S(1)}) custom-call(s32[1,1,24]{2,1,0:T(1,128)S(1)} %copy-done.9, s32[1,1]{1,0:T(1,128)S(6)} %copy.15.live, bf16[1024,512]{1,0:T(8,128)(2,1)S(1)} %copy-done.2, bf16[1024,640]{1,0:T(8,128)(2,1)S(1)} %copy-done, ...), custom_call_target="tpu_custom_call" | custom-call | tf_op jit(solution)/shard_map/attention/pallas_call | solution.py:400
  56.7 0.0 copy-start.1
  56.8 1.0 %copy-done.1 = bf16[1024,512]{1,0:T(8,128)(2,1)} copy-done((bf16[1024,512]{1,0:T(8,128)(2,1)}, bf16[1024,512]{1,0:T(8,128)(2,1)S(1)}, u32[]{:S(2)}) %copy-start.1) | copy-done | bytes 1048600
  57.7 0.8 copy-done.3
  58.5 0.8 copy-done.4
  59.3 26.3 %scatter.1 = (bf16[32,512]{1,0:T(8,128)(2,1)}, bf16[32,512]{1,0:T(8,128)(2,1)}, bf16[32,512]{1,0:T(8,128)(2,1)}) custom-call(bf16[1024,512]{1,0:T(8,128)(2,1)} %copy-done.1, bf16[512,512]{1,0:T(8,128)(2,1)} %copy-done.3, bf16[512,512]{1,0:T(8,128)(2,1)} %copy-done.4), custom_call_target="tpu_custom_call" | custom-call | tf_op jit(solution)/shard_map/scatter/pallas_call | solution.py:311
  85.7 1.4 %copy.16 = bf16[1,32,512]{2,1,0:T(8,128)(2,1)} copy(bf16[1,32,512]{2,1,0:T(8,128)(2,1)} %bitcast.19) | data formatting | bytes 65536
  87.1 1.4 %copy.17 = bf16[1,32,512]{2,1,0:T(8,128)(2,1)} copy(bf16[1,32,512]{2,1,0:T(8,128)(2,1)} %bitcast.18) | data formatting | bytes 65536
  88.4 1.4 %copy.18 = bf16[1,32,512]{2,1,0:T(8,128)(2,1)} copy(bf16[1,32,512]{2,1,0:T(8,128)(2,1)} %bitcast.17) | data formatting | bytes 65536
  (2 shorter events, 0.0 us)
Async XLA Ops:
  37.7 1.3 %copy-start = (bf16[1024,640]{1,0:T(8,128)(2,1)S(1)}, bf16[1024,640]{1,0:T(8,128)(2,1)}, u32[]{:S(2)}) copy-start(bf16[1024,640]{1,0:T(8,128)(2,1)} %get-tuple-element.14.g) | copy-start | bytes 3932164
  39.0 1.2 %copy-start.2 = (bf16[1024,512]{1,0:T(8,128)(2,1)S(1)}, bf16[1024,512]{1,0:T(8,128)(2,1)}, u32[]{:S(2)}) copy-start(bf16[1024,512]{1,0:T(8,128)(2,1)} %get-tuple-element.13.q) | copy-start | bytes 3145732
  40.2 1.0 %copy-start.5 = (bf16[512,512]{1,0:T(8,128)(2,1)S(1)}, bf16[512,512]{1,0:T(8,128)(2,1)}, u32[]{:S(2)}) copy-start(bf16[512,512]{1,0:T(8,128)(2,1)} %get-tuple-element.15.k) | copy-start | bytes 1572868
  41.3 1.0 %copy-start.6 = (bf16[512,512]{1,0:T(8,128)(2,1)S(1)}, bf16[512,512]{1,0:T(8,128)(2,1)}, u32[]{:S(2)}) copy-start(bf16[512,512]{1,0:T(8,128)(2,1)} %get-tuple-element.16.v) | copy-start | bytes 1572868
  42.3 0.9 copy-start.7
  43.2 0.8 copy-start.8
  44.0 0.7 copy-start.9
  56.7 1.0 %copy-start.1 = (bf16[1024,512]{1,0:T(8,128)(2,1)}, bf16[1024,512]{1,0:T(8,128)(2,1)S(1)}, u32[]{:S(2)}) copy-start(bf16[1024,512]{1,0:T(8,128)(2,1)S(1)} %get-tuple-element.17.dq) | copy-start | bytes 3145732
  57.7 0.8 copy-start.3
  58.5 0.8 copy-start.4

commit v2 on v0

v2 whole, which is shorter than its diff:
```python
import functools
import math

import jax
import jax.numpy as jnp
from jax import lax
from jax.experimental import pallas as pl
from jax.experimental.pallas import tpu as pltpu
from jax.sharding import PartitionSpec as P

MESH = pl.DeviceIdType.MESH
RING = 8
PIECE = 32
NEG = -1e30
F32 = jnp.float32
BF16 = jnp.bfloat16


def places():
    r, col = lax.axis_index("row"), lax.axis_index("col")
    xl, z = r // RING, lax.rem(r, RING)
    c = lax.rem(col, 2)
    y = lax.rem(col // 2, RING)
    xh = col // (2 * RING)
    return xl, z, xh, y, c


def turn(a, d):
    return lax.rem(a + d + RING, RING)


def piece(n):
    return pl.ds(pl.multiple_of(n * PIECE, PIECE), PIECE)


def q_rows(xh, y, c):
    return pl.ds(pl.multiple_of((xh * 16 + y * 2 + c) * PIECE, PIECE), PIECE)


def k_rows(xl, z):
    return pl.ds(pl.multiple_of((xl * 8 + z) * PIECE, PIECE), PIECE)


def neighbours(xl, z, xh, y, c):
    def on_col(xh, y, c):
        return {"col": xh * 16 + y * 2 + c}

    def on_row(xl, z):
        return {"row": xl * 8 + z}

    return {
        "qx": on_col(1 - xh, y, c),
        "qc": on_col(xh, y, 1 - c),
        "q+": on_col(xh, turn(y, 1), c),
        "q-": on_col(xh, turn(y, -1), c),
        "kx": on_row(1 - xl, z),
        "k+": on_row(xl, turn(z, 1)),
        "k-": on_row(xl, turn(z, -1)),
    }


def greet(near):
    barrier = pltpu.get_barrier_semaphore()
    for where in near.values():
        pl.semaphore_signal(barrier, inc=1, device_id=where, device_id_type=MESH)
    pl.semaphore_wait(barrier, len(near))


class Post:
    def __init__(self, send, recv):
        self.send, self.recv, self.count, self.sent = send, recv, 0, []

    def slot(self):
        self.count += 1
        return self.count - 1

    def put(self, slot, src, dst, where):
        copy = pltpu.make_async_remote_copy(
            src_ref=src,
            dst_ref=dst,
            send_sem=self.send.at[slot],
            recv_sem=self.recv.at[slot],
            device_id=where,
            device_id_type=MESH,
        )
        copy.start()
        self.sent.append(copy)

    def got(self, slot, dst):
        pltpu.make_async_copy(dst, dst, self.recv.at[slot]).wait()

    def finish(self):
        for copy in self.sent:
            copy.wait_send()


def fused_kernel(
    q, g, o, k, v, lse_in, slots_in, live_in, bits_in,
    oq, ok, ov,
    qa, ga, ka, va, o_s, lse, bits, slots, live,
    bias, delta_t, qt, gt, kc, vc, kt, prob, score,
    dqp, dkv, core_land, kv_land, kv_mine, q_land, q_mine,
    kv_keep, q_keep, kv_out, kv_mate, q_out, q_mate,
    load_sem, send, recv,
):
    xl, z, xh, y, c = places()
    near = neighbours(xl, z, xh, y, c)
    rows, keys = qa.shape[1], ka.shape[1]
    scale = 0.125

    my_q, my_k = q_rows(xh, y, c), k_rows(xl, z)
    loads = {}

    def load(name, pairs):
        made = []
        for src, dst in pairs:
            copy = pltpu.make_async_copy(src, dst, load_sem.at[load.count])
            load.count += 1
            copy.start()
            made.append(copy)
        loads[name] = made

    def loaded(*names):
        for name in names:
            for copy in loads[name]:
                copy.wait()

    load.count = 0
    for name, src, full, where in (("k", k, ka, my_k), ("q", q, qa, my_q), ("v", v, va, my_k), ("g", g, ga, my_q)):
        load(name, [(src.at[:, p * 128 : p * 128 + 128], full.at[p, where, :]) for p in range(4)])
    load("o", [(o.at[:, p * 128 : p * 128 + 128], o_s.at[p]) for p in range(4)])
    load("tables", [(slots_in, slots), (live_in, live), (bits_in, bits)])
    load("lse", [(lse_in, lse)])

    greet(near)
    post = Post(send, recv)

    streams = {}
    for name, kind, full, place, reach in (
        ("k", "k", ka, (xl, z), ((1, 4), (-1, 3))),
        ("q", "q", qa, (xh, y), ((1, 4), (-1, 3))),
        ("v", "k", va, (xl, z), ((1, 3), (-1, 4))),
        ("g", "q", ga, (xh, y), ((1, 3), (-1, 4))),
    ):
        st = dict(kind=kind, full=full, pos=place[0], ring=place[1], reach=reach, slots={}, core={})
        st["rows"] = q_rows if kind == "q" else (lambda x, t, core: k_rows(x, t))
        st["mate"] = post.slot()
        for s in range(2):
            shifts = [0]
            for sign, far in reach:
                for d in range(1, far + 1):
                    st["slots"][s, sign, d] = post.slot()
                    shifts.append(sign * d)
            if kind == "q":
                for shift in shifts:
                    st["core"][s, shift] = post.slot()
        streams[name] = st

    def piece_of(st, s, shift, core):
        pos = st["pos"] if s == 0 else 1 - st["pos"]
        return st["full"].at[:, st["rows"](pos, turn(st["ring"], -shift), core), :]

    def ring_send(st, s, sign, d):
        ref = piece_of(st, s, sign * (d - 1), c)
        post.put(st["slots"][s, sign, d], ref, ref, near[st["kind"] + ("+" if sign > 0 else "-")])

    def core_send(st, s, shift):
        if st["kind"] == "q":
            ref = piece_of(st, s, shift, c)
            post.put(st["core"][s, shift], ref, ref, near["qc"])

    def begin(st):
        ref = piece_of(st, 0, 0, c)
        post.put(st["mate"], ref, ref, near[st["kind"] + "x"])
        for sign, _ in st["reach"]:
            ring_send(st, 0, sign, 1)
        core_send(st, 0, 0)

    def relay(st, s, d):
        for sign, far in st["reach"]:
            if d <= far:
                post.got(st["slots"][s, sign, d], piece_of(st, s, sign * d, c))
                if d < far:
                    ring_send(st, s, sign, d + 1)
                core_send(st, s, sign * d)

    def relay_mate(st):
        post.got(st["mate"], piece_of(st, 1, 0, c))
        for sign, _ in st["reach"]:
            ring_send(st, 1, sign, 1)
        core_send(st, 1, 0)

    for name in ("k", "q", "v"):
        loaded(name)
        begin(streams[name])
    loaded("g", "o")
    lane = lax.broadcasted_iota(jnp.int32, (PIECE, 128), 1)
    delta = jnp.zeros((PIECE, 128), F32)
    for p in range(4):
        product = ga[p, my_q, :].astype(F32) * o_s[p].astype(F32)
        for a in range(2):
            one = jnp.sum(product[:, a * 64 : a * 64 + 64], axis=1, keepdims=True)
            delta = jnp.where(lane == 2 * p + a, one, delta)
    ga[4, my_q, :] = delta.astype(BF16)
    begin(streams["g"])

    loaded("tables")
    bit_of = lax.broadcasted_iota(jnp.int32, (16, 128), 0)
    listed = live[0, 0]

    @pl.loop(0, 32)
    def _(t):
        entry, valid = jnp.int32(0), jnp.int32(0)
        for e in range(24):
            hit = jnp.logical_and(slots[0, 0, e] == t, e < listed)
            entry = jnp.where(hit, jnp.int32(e), entry)
            valid = jnp.where(hit, jnp.int32(1), valid)
        words = bits[entry] * valid
        across = pl.multiple_of((t // 4) * 128, 128)
        down = pl.multiple_of(lax.rem(t, 4) * 128, 128)
        for r in range(8):
            word = jnp.broadcast_to(words[r : r + 1, :], (16, 128))
            edge = jnp.bitwise_and(jnp.right_shift(word, bit_of), 1)
            bias[pl.ds(down + r * 16, 16), pl.ds(across, 128)] = jnp.where(edge == 1, 0.0, NEG)

    names = ("k", "q", "v", "g")
    for d in range(1, 6):
        if d <= 4:
            for n in names:
                relay(streams[n], 0, d)
        for n in names:
            if d == 1:
                relay_mate(streams[n])
            else:
                relay(streams[n], 1, d - 1)
    for n in ("q", "g"):
        st = streams[n]
        for (s, shift), slot in st["core"].items():
            post.got(slot, piece_of(st, s, shift, 1 - c))
    loaded("lse")

    for p in range(4):
        pass
    book = [
        dict(core=post.slot(), kv=[[post.slot() for _ in range(4)] for _ in range(2)],
             q=[[post.slot() for _ in range(4)] for _ in range(2)], kvm=post.slot(), qm=post.slot())
        for _ in range(4)
    ]
    signs = ((0, 1), (1, -1))

    def kv_send(p, si, s, src, dst):
        post.put(book[p]["kv"][si][s], src, dst, near["k+" if si == 0 else "k-"])

    def scatter_start(p):
        post.put(book[p]["core"], dqp.at[p, :, :, 1 - c], core_land.at[p], near["qc"])
        far = piece(turn(z, 4))
        for si, _ in signs:
            half = slice(2 * si, 2 * si + 2)
            kv_send(p, si, 0, dkv.at[p, half, far, :], kv_land.at[p, si, 0, half])

    def kv_step(p, s):
        for si, sign in signs:
            half = slice(2 * si, 2 * si + 2)
            mine = piece(turn(z, sign * (4 - s)))
            if s == 1:
                post.got(book[p]["kv"][si][0], kv_land.at[p, si, 0, half])
                kv_mine[p, si, 1] = dkv[p, :, mine, :]
                kv_mine[p, si, 1, half] = (
                    dkv[p, half, mine, :].astype(F32) + kv_land[p, si, 0, half].astype(F32)
                ).astype(BF16)
            else:
                post.got(book[p]["kv"][si][s - 1], kv_land.at[p, si, s - 1])
                kv_mine[p, si, s] = (
                    dkv[p, :, mine, :].astype(F32) + kv_land[p, si, s - 1].astype(F32)
                ).astype(BF16)
            kv_send(p, si, s, kv_mine.at[p, si, s], kv_land.at[p, si, s])

    def q_own(p, t):
        return dqp[p, :, t, c].astype(F32) + core_land[p, :, t].astype(F32)

    def q_step(p, s):
        if s == 0:
            post.got(book[p]["core"], core_land.at[p])
        for si, sign in signs:
            t = turn(y, sign * (4 - s))
            way = near["q+" if si == 0 else "q-"]
            if s == 0:
                total = dqp[p, si, t, c].astype(F32) + core_land[p, si, t].astype(F32)
                q_mine[p, si, 0, si] = total.astype(BF16)
                post.put(book[p]["q"][si][0], q_mine.at[p, si, 0, si], q_land.at[p, si, 0, si], way)
                continue
            total = q_own(p, t)
            if s == 1:
                post.got(book[p]["q"][si][0], q_land.at[p, si, 0, si])
                q_mine[p, si, 1, 1 - si] = total[1 - si].astype(BF16)
                q_mine[p, si, 1, si] = (total[si] + q_land[p, si, 0, si].astype(F32)).astype(BF16)
            else:
                post.got(book[p]["q"][si][s - 1], q_land.at[p, si, s - 1])
                q_mine[p, si, s] = (total + q_land[p, si, s - 1].astype(F32)).astype(BF16)
            post.put(book[p]["q"][si][s], q_mine.at[p, si, s], q_land.at[p, si, s], way)

    def kv_final(p):
        total = dkv[p, :, piece(z), :].astype(F32)
        for si, _ in signs:
            post.got(book[p]["kv"][si][3], kv_land.at[p, si, 3])
            total = total + kv_land[p, si, 3].astype(F32)
        for n in range(2):
            kv_keep[p, n] = jnp.where(xl == 0, total[2 * n], total[2 * n + 1])
            kv_out[p, n] = jnp.where(xl == 0, total[2 * n + 1], total[2 * n]).astype(BF16)
        post.put(book[p]["kvm"], kv_out.at[p], kv_mate.at[p], near["kx"])

    def q_final(p):
        total = q_own(p, y)
        for si, _ in signs:
            post.got(book[p]["q"][si][3], q_land.at[p, si, 3])
            total = total + q_land[p, si, 3].astype(F32)
        q_keep[p] = jnp.where(xh == 0, total[0], total[1])
        q_out[p] = jnp.where(xh == 0, total[1], total[0]).astype(BF16)
        post.put(book[p]["qm"], q_out.at[p], q_mate.at[p], near["qx"])

    def kv_done(p):
        post.got(book[p]["kvm"], kv_mate.at[p])
        for n, out in enumerate((ok, ov)):
            out[:, p * 128 : p * 128 + 128] = (kv_keep[p, n] + kv_mate[p, n].astype(F32)).astype(BF16)

    def q_done(p):
        post.got(book[p]["qm"], q_mate.at[p])
        oq[:, p * 128 : p * 128 + 128] = (q_keep[p] + q_mate[p].astype(F32)).astype(BF16)

    turns = {
        "kv": [functools.partial(kv_step, s=s) for s in range(1, 4)] + [kv_final, kv_done],
        "q": [functools.partial(q_step, s=s) for s in range(4)] + [q_final, q_done],
    }
    at = {(kind, p): 0 for kind in turns for p in range(4)}

    def advance(kind, p):
        n = at[kind, p]
        if 0 <= p and n < len(turns[kind]):
            turns[kind][n](p)
            at[kind, p] = n + 1
            return True
        return False

    delta_t[...] = ga[4].astype(F32).T
    lane = lax.broadcasted_iota(jnp.int32, (keys, 128), 1)
    row = lax.broadcasted_iota(jnp.int32, (16, rows), 0)
    for p in range(4):
        kp = ka[p].astype(F32)
        vp = va[p].astype(F32)
        qp_t = qa[p].T
        gp_t = ga[p].T
        kt[...] = ka[p].T
        for a in range(2):
            own = (lane < 64) if a == 0 else (lane >= 64)
            free = 64 * (1 - a)
            kc[a] = jnp.where(own, kp, jnp.where(lane < free + 3, 1.0, 0.0)).astype(BF16)
            vc[a] = jnp.where(own, vp, jnp.where(lane < free + 1, 1.0, 0.0)).astype(BF16)
            low = lse[2 * p + a : 2 * p + a + 1, :] * (-8.0)
            first = low.astype(BF16).astype(F32)
            second = (low - first).astype(BF16).astype(F32)
            third = low - first - second
            qt[a] = qp_t
            qt[a, free : free + 16, :] = jnp.where(
                row == 0, first, jnp.where(row == 1, second, jnp.where(row == 2, third, 0.0))
            ).astype(BF16)
            gt[a] = gp_t
            gt[a, free : free + 16, :] = jnp.where(
                row == 0, -delta_t[2 * p + a : 2 * p + a + 1, :], 0.0
            ).astype(BF16)
        parts = []
        for a in range(2):
            for ib in range(rows // 256):
                for jb in range(keys // 128):
                    js, is_ = slice(jb * 128, jb * 128 + 128), slice(ib * 256, ib * 256 + 256)
                    s = jnp.dot(kc[a, js, :], qt[a, :, is_], preferred_element_type=F32)
                    w = jnp.dot(vc[a, js, :], gt[a, :, is_], preferred_element_type=F32)
                    pr = jnp.exp2(s * (scale * math.log2(math.e)) + bias[js, is_])
                    prob[js, is_] = pr.astype(BF16)
                    score[js, is_] = (pr * w).astype(BF16)
            value_sum = jnp.dot(prob[...], ga[p], preferred_element_type=F32)
            key_sum = jnp.dot(score[...], qa[p], preferred_element_type=F32)
            query_sum = jnp.dot(kt[64 * a : 64 * a + 64, :], score[...], preferred_element_type=F32)
            parts.append((value_sum, key_sum, query_sum))
            if a == 0:
                for back in range(1, 4):
                    if p >= back:
                        advance("q", p - back)
        dkv[p, 0:2] = (jnp.where(lane < 64, parts[0][1], parts[1][1]) * scale).astype(BF16).reshape(2, 256, 128)
        dkv[p, 2:4] = jnp.where(lane < 64, parts[0][0], parts[1][0]).astype(BF16).reshape(2, 256, 128)
        both = jnp.concatenate([parts[0][2], parts[1][2]], axis=0) * scale
        dqp[p] = both.T.astype(BF16).reshape(2, 8, 2, PIECE, 128)
        scatter_start(p)
        for back in range(1, 4):
            if p >= back:
                advance("kv", p - back)
    busy = True
    while busy:
        busy = False
        for p in range(4):
            for kind in ("kv", "q"):
                busy = advance(kind, p) or busy
    post.finish()


COPIES = 2 * 15 + 2 * (15 + 16) + 4 * 19


def fused(q, g, o, k, v, lse, slots, live, bits):
    vmem = pl.BlockSpec(memory_space=pltpu.VMEM)
    hbm = pl.BlockSpec(memory_space=pl.ANY)
    rows, keys = 1024, 512
    return pl.pallas_call(
        fused_kernel,
        out_shape=[jax.ShapeDtypeStruct((PIECE, 512), BF16)] * 3,
        in_specs=[hbm] * 9,
        out_specs=[vmem] * 3,
        scratch_shapes=[
            pltpu.VMEM((4, rows, 128), BF16),
            pltpu.VMEM((5, rows, 128), BF16),
            pltpu.VMEM((4, keys, 128), BF16),
            pltpu.VMEM((4, keys, 128), BF16),
            pltpu.VMEM((4, PIECE, 128), BF16),
            pltpu.VMEM(lse.shape, F32),
            pltpu.VMEM(bits.shape, jnp.int32),
            pltpu.SMEM(slots.shape, jnp.int32),
            pltpu.SMEM(live.shape, jnp.int32),
            pltpu.VMEM((keys, rows), F32),
            pltpu.VMEM((128, rows), F32),
            pltpu.VMEM((2, 128, rows), BF16),
            pltpu.VMEM((2, 128, rows), BF16),
            pltpu.VMEM((2, keys, 128), BF16),
            pltpu.VMEM((2, keys, 128), BF16),
            pltpu.VMEM((128, keys), BF16),
            pltpu.VMEM((keys, rows), BF16),
            pltpu.VMEM((keys, rows), BF16),
            pltpu.VMEM((4, 2, 8, 2, PIECE, 128), BF16),
            pltpu.VMEM((4, 4, 256, 128), BF16),
            pltpu.VMEM((4, 2, 8, PIECE, 128), BF16),
            pltpu.VMEM((4, 2, 4, 4, PIECE, 128), BF16),
            pltpu.VMEM((4, 2, 4, 4, PIECE, 128), BF16),
            pltpu.VMEM((4, 2, 4, 2, PIECE, 128), BF16),
            pltpu.VMEM((4, 2, 4, 2, PIECE, 128), BF16),
            pltpu.VMEM((4, 2, PIECE, 128), F32),
            pltpu.VMEM((4, PIECE, 128), F32),
            pltpu.VMEM((4, 2, PIECE, 128), BF16),
            pltpu.VMEM((4, 2, PIECE, 128), BF16),
            pltpu.VMEM((4, PIECE, 128), BF16),
            pltpu.VMEM((4, PIECE, 128), BF16),
            pltpu.SemaphoreType.DMA((24,)),
            pltpu.SemaphoreType.DMA((COPIES,)),
            pltpu.SemaphoreType.DMA((COPIES,)),
        ],
        compiler_params=pltpu.CompilerParams(
            collective_id=0, has_side_effects=True, vmem_limit_bytes=56 << 20
        ),
        name="fused",
    )(q, g, o, k, v, lse, slots, live, bits)


def body(queries, keys, values, outputs, grad_out, lse, tile_slot, tile_live, tile_bits):
    oq, ok, ov = fused(
        queries[0], grad_out[0], outputs[0], keys[0], values[0], lse[0], tile_slot, tile_live, tile_bits[0, 0]
    )
    return oq[None], ok[None], ov[None]


def solution(mesh):
    in_specs = (
        P("row", "col", None),
        P("col", "row", None),
        P("col", "row", None),
        P("row", "col", None),
        P("row", "col", None),
        P("row", None, None),
        P("row", "col", None),
        P("row", "col"),
        P("row", "col", None, None, None),
    )
    out_specs = (P("row", "col", None), P("col", "row", None), P("col", "row", None))
    return jax.shard_map(body, mesh=mesh, in_specs=in_specs, out_specs=out_specs, check_vma=False)
```

time: 921 us -> 77.3 us (0.08)
  the two profiles are of different devices: /device:TPU:1 before, /device:TPU:8 now
where the time goes in v2:
time: 77.3 us; the launch traced here: 77 us
  Pallas kernels  72.9 us (94%)
  local copies, waits for them, and re-layouts  2.77 us (4%)
  between operations  1.3 us (2%)
    pallas_call x1, Pallas kernels, fused(): pl.pallas_call(fused_kernel, out_shape=[jax.ShapeDtypeStruct((PIECE, 512)...  72.9 us
    unnamed x7, local copies, waits for them, and re-layouts  2.77 us

profile of v2, /device:TPU:8, one launch (start us, length us, event | category | flops | bytes accessed | tf_op | source)
XLA Modules:
  0.0 77.0 jit_solution(3967192481169699651)
XLA Ops:
  1.3 72.9 %fused.1 = (bf16[32,512]{1,0:T(8,128)(2,1)}, bf16[32,512]{1,0:T(8,128)(2,1)}, bf16[32,512]{1,0:T(8,128)(2,1)}) custom-call(bf16[32,512]{1,0:T(8,128)(2,1)} %bitcast.11, bf16[32,512]{1,0:T(8,128)(2,1)} %bitcast.12, bf16[32,512]{1,0:T(8,128)(2,1)} %bitcast.13, bf16[32,512]{1,0:T(8,128)(2,1)} %bitcast.14, bf16[32,512]{1,0:T(8,128)(2,1)} %bitcast.15, ...), custom_call_target="tpu_custom_call" | custom-call | tf_op jit(solution)/shard_map/fused/pallas_call | solution.py:412
  74.2 0.0 copy-start.1
  74.2 1.4 %copy.16 = bf16[1,32,512]{2,1,0:T(8,128)(2,1)} copy(bf16[1,32,512]{2,1,0:T(8,128)(2,1)} %bitcast.19) | data formatting | bytes 65536
  75.6 0.0 copy-done.1
  75.6 0.0 copy-start
  75.6 0.6 copy.17
  76.2 0.2 copy-done
  76.4 0.6 copy.18
Async XLA Ops:
  74.2 1.4 %copy-start.1 = (bf16[32,512]{1,0:T(8,128)(2,1)S(1)}, bf16[32,512]{1,0:T(8,128)(2,1)}, u32[]{:S(2)}) copy-start(bf16[32,512]{1,0:T(8,128)(2,1)} %get-tuple-element.7) | copy-start | bytes 98308
  75.6 0.8 %copy-start = (bf16[32,512]{1,0:T(8,128)(2,1)S(1)}, bf16[32,512]{1,0:T(8,128)(2,1)}, u32[]{:S(2)}) copy-start(bf16[32,512]{1,0:T(8,128)(2,1)} %get-tuple-element.8) | copy-start | bytes 98308

commit v3 on v2

v3 whole, which is shorter than its diff:
```python
import functools
import math

import jax
import jax.numpy as jnp
from jax import lax
from jax.experimental import pallas as pl
from jax.experimental.pallas import tpu as pltpu
from jax.sharding import PartitionSpec as P

MESH = pl.DeviceIdType.MESH
RING = 8
PIECE = 32
NEG = -1e30
F32 = jnp.float32
BF16 = jnp.bfloat16


def places():
    r, col = lax.axis_index("row"), lax.axis_index("col")
    xl, z = r // RING, lax.rem(r, RING)
    c = lax.rem(col, 2)
    y = lax.rem(col // 2, RING)
    xh = col // (2 * RING)
    return xl, z, xh, y, c


def turn(a, d):
    return lax.rem(a + d + RING, RING)


def piece(n):
    return pl.ds(pl.multiple_of(n * PIECE, PIECE), PIECE)


def q_rows(xh, y, c):
    return pl.ds(pl.multiple_of((xh * 16 + y * 2 + c) * PIECE, PIECE), PIECE)


def k_rows(xl, z):
    return pl.ds(pl.multiple_of((xl * 8 + z) * PIECE, PIECE), PIECE)


CHAIN = {1: 0, 2: 1, 3: 2, 4: 3, -1: 0, -2: -1, -3: -2}
DEEP = {1: 0, 2: 0, 3: 2, 4: 3, -1: 0, -2: -1, -3: -2}
FLAT = {1: 0, 2: 1, 3: 0, 4: 3, -1: 0, -2: 0, -3: -2}


def mirror(tree):
    return {-child: -parent for child, parent in tree.items()}


def neighbours(xl, z, xh, y, c):
    near = {"core": {"col": xh * 16 + y * 2 + 1 - c}}
    for far in range(-3, 4):
        for other in range(2):
            if far == 0 and other == 0:
                continue
            x = 1 - xh if other else xh
            near["q", other, far] = {"col": x * 16 + turn(y, far) * 2 + c}
            x = 1 - xl if other else xl
            near["k", other, far] = {"row": x * 8 + turn(z, far)}
    return near


def greet(near):
    barrier = pltpu.get_barrier_semaphore()
    for where in near.values():
        pl.semaphore_signal(barrier, inc=1, device_id=where, device_id_type=MESH)
    pl.semaphore_wait(barrier, len(near))


class Post:
    def __init__(self, send, recv):
        self.send, self.recv, self.count, self.sent = send, recv, 0, []

    def slot(self):
        self.count += 1
        return self.count - 1

    def put(self, slot, src, dst, where):
        copy = pltpu.make_async_remote_copy(
            src_ref=src,
            dst_ref=dst,
            send_sem=self.send.at[slot],
            recv_sem=self.recv.at[slot],
            device_id=where,
            device_id_type=MESH,
        )
        copy.start()
        self.sent.append(copy)

    def got(self, slot, dst):
        pltpu.make_async_copy(dst, dst, self.recv.at[slot]).wait()

    def finish(self):
        for copy in self.sent:
            copy.wait_send()


OWN_TREE, MATE_TREE = CHAIN, FLAT


def fused_kernel(
    q, g, o, k, v, lse_in, slots_in, live_in, bits_in,
    oq, ok, ov,
    qa, ga, ka, va, o_s, lse, bits, slots, live,
    bias, delta_t, qt, gt, kc, vc, kt, prob, score,
    dqp, dkv, core_land, kv_leaf, kv_mine, kv_root, q_leaf, q_mine, q_root,
    load_sem, send, recv,
):
    xl, z, xh, y, c = places()
    near = neighbours(xl, z, xh, y, c)
    rows, keys = qa.shape[1], ka.shape[1]
    scale = 0.125

    my_q, my_k = q_rows(xh, y, c), k_rows(xl, z)
    loads = {}

    def load(name, pairs):
        made = []
        for src, dst in pairs:
            copy = pltpu.make_async_copy(src, dst, load_sem.at[load.count])
            load.count += 1
            copy.start()
            made.append(copy)
        loads[name] = made

    def loaded(*names):
        for name in names:
            for copy in loads[name]:
                copy.wait()

    load.count = 0
    for name, src, full, where in (("k", k, ka, my_k), ("q", q, qa, my_q), ("v", v, va, my_k), ("g", g, ga, my_q)):
        load(name, [(src.at[:, p * 128 : p * 128 + 128], full.at[p, where, :]) for p in range(4)])
    load("o", [(o.at[:, p * 128 : p * 128 + 128], o_s.at[p]) for p in range(4)])
    load("tables", [(slots_in, slots), (live_in, live), (bits_in, bits)])
    load("lse", [(lse_in, lse)])

    greet(near)
    post = Post(send, recv)

    streams = {}
    for name, kind, full, place, flip in (
        ("k", "k", ka, (xl, z), False),
        ("q", "q", qa, (xh, y), False),
        ("v", "k", va, (xl, z), True),
        ("g", "q", ga, (xh, y), True),
    ):
        trees = [mirror(t) if flip else t for t in (OWN_TREE, MATE_TREE)]
        st = dict(kind=kind, full=full, pos=place[0], ring=place[1], trees=trees, slots={}, core={}, mate=post.slot())
        st["rows"] = q_rows if kind == "q" else (lambda x, t, core: k_rows(x, t))
        for s in range(2):
            for d in trees[s]:
                st["slots"][s, d] = post.slot()
            if kind == "q":
                for d in (0, *trees[s]):
                    st["core"][s, d] = post.slot()
        streams[name] = st

    def piece_of(st, s, shift, core):
        pos = st["pos"] if s == 0 else 1 - st["pos"]
        return st["full"].at[:, st["rows"](pos, turn(st["ring"], -shift), core), :]

    def pass_on(st, s, d):
        ref = piece_of(st, s, d, c)
        for child, parent in sorted(st["trees"][s].items(), key=lambda e: -abs(e[0] - e[1])):
            if parent == d:
                post.put(st["slots"][s, child], ref, ref, near[st["kind"], 0, child - parent])
        if st["kind"] == "q":
            post.put(st["core"][s, d], ref, ref, near["core"])

    def begin(st):
        ref = piece_of(st, 0, 0, c)
        post.put(st["mate"], ref, ref, near[st["kind"], 1, 0])
        pass_on(st, 0, 0)

    def arrive(st, s, d):
        if (s, d) == (1, 0):
            post.got(st["mate"], piece_of(st, 1, 0, c))
        else:
            post.got(st["slots"][s, d], piece_of(st, s, d, c))
        pass_on(st, s, d)

    def arrivals():
        found = []
        for n, name in enumerate(("k", "q", "v", "g")):
            st = streams[name]
            for s in range(2):
                first = 0.0 if s == 0 else (2.6 if st["kind"] == "k" else 3.6)
                first += 0.4 * n + (1.5 if name == "g" else 0.0)
                if s == 1:
                    found.append((first, name, 1, 0))
                for d in st["trees"][s]:
                    when, at_d = first, d
                    while at_d != 0:
                        up = st["trees"][s][at_d]
                        when += 2.9 + 0.6 * (abs(at_d - up) - 1)
                        at_d = up
                    found.append((when, name, s, d))
        return sorted(found)

    for name in ("k", "q", "v"):
        loaded(name)
        begin(streams[name])
    loaded("g", "o")
    lane = lax.broadcasted_iota(jnp.int32, (PIECE, 128), 1)
    delta = jnp.zeros((PIECE, 128), F32)
    for p in range(4):
        product = ga[p, my_q, :].astype(F32) * o_s[p].astype(F32)
        for a in range(2):
            one = jnp.sum(product[:, a * 64 : a * 64 + 64], axis=1, keepdims=True)
            delta = jnp.where(lane == 2 * p + a, one, delta)
    ga[4, my_q, :] = delta.astype(BF16)
    begin(streams["g"])

    loaded("tables")
    bit_of = lax.broadcasted_iota(jnp.int32, (16, 128), 0)
    listed = live[0, 0]

    @pl.loop(0, 32)
    def _(t):
        entry, valid = jnp.int32(0), jnp.int32(0)
        for e in range(24):
            hit = jnp.logical_and(slots[0, 0, e] == t, e < listed)
            entry = jnp.where(hit, jnp.int32(e), entry)
            valid = jnp.where(hit, jnp.int32(1), valid)
        words = bits[entry] * valid
        across = pl.multiple_of((t // 4) * 128, 128)
        down = pl.multiple_of(lax.rem(t, 4) * 128, 128)
        for r in range(8):
            word = jnp.broadcast_to(words[r : r + 1, :], (16, 128))
            edge = jnp.bitwise_and(jnp.right_shift(word, bit_of), 1)
            bias[pl.ds(down + r * 16, 16), pl.ds(across, 128)] = jnp.where(edge == 1, 0.0, NEG)

    for _, name, s, d in arrivals():
        arrive(streams[name], s, d)
    for n in ("q", "g"):
        st = streams[n]
        for (s, shift), slot in st["core"].items():
            post.got(slot, piece_of(st, s, shift, 1 - c))
    loaded("lse")

    trees = (FLAT, mirror(FLAT))
    leaves = [[d for d in t if d not in t.values() and t[d] != 0] for t in trees]
    tops = [[d for d in t if t[d] == 0] for t in trees]
    book = []
    for p in range(4):
        entry = dict(core=post.slot())
        for kind in ("kv", "q"):
            for n in range(2):
                for d in leaves[n]:
                    entry[kind, n, "leaf", d] = post.slot()
                for b in range(2) if kind == "kv" else (n,):
                    for d in tops[n] + ([0] if b == 1 else []):
                        entry[kind, n, b, d] = post.slot()
        book.append(entry)

    def child_of(n, d):
        found = [e for e, up in trees[n].items() if up == d]
        return found[0] if found else None

    def kv_top(p, n, b, d, src):
        dst = kv_root.at[p, n, b, tops[n].index(d) if d else 4]
        post.put(book[p]["kv", n, b, d], src, dst, near["k", b, -d])

    def kv_side(b):
        return xl if b == 0 else 1 - xl

    def scatter_start(p):
        post.put(book[p]["core"], dqp.at[p, :, :, 1 - c], core_land.at[p], near["core"])
        for n in range(2):
            for i, d in enumerate(leaves[n]):
                src = dkv.at[p, 2 * n : 2 * n + 2, piece(turn(z, -d)), :]
                post.put(book[p]["kv", n, "leaf", d], src, kv_leaf.at[p, n, i], near["k", 0, trees[n][d] - d])
            for d in tops[n]:
                if child_of(n, d) is None:
                    for b in range(2):
                        kv_top(p, n, b, d, dkv.at[p, 2 * n + kv_side(b), piece(turn(z, -d)), :])
            kv_top(p, n, 1, 0, dkv.at[p, 2 * n + kv_side(1), piece(z), :])

    def kv_middle(p):
        for n in range(2):
            for j, d in enumerate(tops[n]):
                e = child_of(n, d)
                if e is None:
                    continue
                i = leaves[n].index(e)
                post.got(book[p]["kv", n, "leaf", e], kv_leaf.at[p, n, i])
                own = dkv[p, 2 * n : 2 * n + 2, piece(turn(z, -d)), :].astype(F32)
                kv_mine[p, n, j] = (own + kv_leaf[p, n, i].astype(F32)).astype(BF16)
                for b in range(2):
                    kv_top(p, n, b, d, kv_mine.at[p, n, j, kv_side(b)])

    def kv_final(p):
        for n, out in enumerate((ok, ov)):
            total = dkv[p, 2 * n + xl, piece(z), :].astype(F32)
            for b in range(2):
                for d in tops[n] + ([0] if b == 1 else []):
                    i = tops[n].index(d) if d else 4
                    post.got(book[p]["kv", n, b, d], kv_root.at[p, n, b, i])
                    total = total + kv_root[p, n, b, i].astype(F32)
            out[:, p * 128 : p * 128 + 128] = total.astype(BF16)

    def q_own(p, b, t):
        side = xh if b == 0 else 1 - xh
        return dqp[p, side, t, c].astype(F32) + core_land[p, side, t].astype(F32)

    def q_put(p, b, d, total):
        i = (leaves[b] + tops[b] + [0]).index(d)
        q_mine[p, b, i] = total.astype(BF16)
        if d in leaves[b]:
            slot, dst = book[p]["q", b, "leaf", d], q_leaf.at[p, b, i]
            post.put(slot, q_mine.at[p, b, i], dst, near["q", 0, trees[b][d] - d])
        else:
            dst = q_root.at[p, b, i - len(leaves[b])]
            post.put(book[p]["q", b, b, d], q_mine.at[p, b, i], dst, near["q", b, -d])

    def q_first(p):
        post.got(book[p]["core"], core_land.at[p])
        for b in range(2):
            for d in leaves[b] + [d for d in tops[b] if child_of(b, d) is None]:
                q_put(p, b, d, q_own(p, b, turn(y, -d)))
        q_put(p, 1, 0, q_own(p, 1, y))

    def q_middle(p):
        for b in range(2):
            for d in tops[b]:
                e = child_of(b, d)
                if e is None:
                    continue
                i = leaves[b].index(e)
                post.got(book[p]["q", b, "leaf", e], q_leaf.at[p, b, i])
                q_put(p, b, d, q_own(p, b, turn(y, -d)) + q_leaf[p, b, i].astype(F32))

    def q_final(p):
        total = q_own(p, 0, y)
        for b in range(2):
            for d in tops[b] + ([0] if b == 1 else []):
                i = tops[b].index(d) if d else 4
                post.got(book[p]["q", b, b, d], q_root.at[p, b, i])
                total = total + q_root[p, b, i].astype(F32)
        oq[:, p * 128 : p * 128 + 128] = total.astype(BF16)

    delta_t[...] = ga[4].astype(F32).T
    lane = lax.broadcasted_iota(jnp.int32, (keys, 128), 1)
    row = lax.broadcasted_iota(jnp.int32, (16, rows), 0)
    for p in range(4):
        kp = ka[p].astype(F32)
        vp = va[p].astype(F32)
        qp_t = qa[p].T
        gp_t = ga[p].T
        kt[...] = ka[p].T
        for a in range(2):
            own = (lane < 64) if a == 0 else (lane >= 64)
            free = 64 * (1 - a)
            kc[a] = jnp.where(own, kp, jnp.where(lane < free + 3, 1.0, 0.0)).astype(BF16)
            vc[a] = jnp.where(own, vp, jnp.where(lane < free + 1, 1.0, 0.0)).astype(BF16)
            low = lse[2 * p + a : 2 * p + a + 1, :] * (-8.0)
            first = low.astype(BF16).astype(F32)
            second = (low - first).astype(BF16).astype(F32)
            third = low - first - second
            qt[a] = qp_t
            qt[a, free : free + 16, :] = jnp.where(
                row == 0, first, jnp.where(row == 1, second, jnp.where(row == 2, third, 0.0))
            ).astype(BF16)
            gt[a] = gp_t
            gt[a, free : free + 16, :] = jnp.where(
                row == 0, -delta_t[2 * p + a : 2 * p + a + 1, :], 0.0
            ).astype(BF16)
        parts = []
        for a in range(2):
            for ib in range(rows // 256):
                for jb in range(keys // 128):
                    js, is_ = slice(jb * 128, jb * 128 + 128), slice(ib * 256, ib * 256 + 256)
                    s = jnp.dot(kc[a, js, :], qt[a, :, is_], preferred_element_type=F32)
                    w = jnp.dot(vc[a, js, :], gt[a, :, is_], preferred_element_type=F32)
                    pr = jnp.exp2(s * (scale * math.log2(math.e)) + bias[js, is_])
                    prob[js, is_] = pr.astype(BF16)
                    score[js, is_] = (pr * w).astype(BF16)
            value_sum = jnp.dot(prob[...], ga[p], preferred_element_type=F32)
            key_sum = jnp.dot(score[...], qa[p], preferred_element_type=F32)
            query_sum = jnp.dot(kt[64 * a : 64 * a + 64, :], score[...], preferred_element_type=F32)
            parts.append((value_sum, key_sum, query_sum))
            if a == 0:
                if p >= 1:
                    q_first(p - 1)
                if p >= 2:
                    kv_middle(p - 2)
        dkv[p, 0:2] = (jnp.where(lane < 64, parts[0][1], parts[1][1]) * scale).astype(BF16).reshape(2, 256, 128)
        dkv[p, 2:4] = jnp.where(lane < 64, parts[0][0], parts[1][0]).astype(BF16).reshape(2, 256, 128)
        both = jnp.concatenate([parts[0][2], parts[1][2]], axis=0) * scale
        dqp[p] = both.T.astype(BF16).reshape(2, 8, 2, PIECE, 128)
        scatter_start(p)
        if p >= 2:
            q_middle(p - 2)
        if p >= 3:
            kv_final(p - 3)
    q_first(3)
    kv_middle(2)
    q_middle(2)
    kv_middle(3)
    q_middle(3)
    for p in range(4):
        if p > 0:
            kv_final(p)
        q_final(p)
    post.finish()


COPIES = 2 * 15 + 2 * (15 + 16) + 4 * 40


def fused(q, g, o, k, v, lse, slots, live, bits):
    vmem = pl.BlockSpec(memory_space=pltpu.VMEM)
    hbm = pl.BlockSpec(memory_space=pl.ANY)
    rows, keys = 1024, 512
    return pl.pallas_call(
        fused_kernel,
        out_shape=[jax.ShapeDtypeStruct((PIECE, 512), BF16)] * 3,
        in_specs=[hbm] * 9,
        out_specs=[vmem] * 3,
        scratch_shapes=[
            pltpu.VMEM((4, rows, 128), BF16),
            pltpu.VMEM((5, rows, 128), BF16),
            pltpu.VMEM((4, keys, 128), BF16),
            pltpu.VMEM((4, keys, 128), BF16),
            pltpu.VMEM((4, PIECE, 128), BF16),
            pltpu.VMEM(lse.shape, F32),
            pltpu.VMEM(bits.shape, jnp.int32),
            pltpu.SMEM(slots.shape, jnp.int32),
            pltpu.SMEM(live.shape, jnp.int32),
            pltpu.VMEM((keys, rows), F32),
            pltpu.VMEM((128, rows), F32),
            pltpu.VMEM((2, 128, rows), BF16),
            pltpu.VMEM((2, 128, rows), BF16),
            pltpu.VMEM((2, keys, 128), BF16),
            pltpu.VMEM((2, keys, 128), BF16),
            pltpu.VMEM((128, keys), BF16),
            pltpu.VMEM((keys, rows), BF16),
            pltpu.VMEM((keys, rows), BF16),
            pltpu.VMEM((4, 2, 8, 2, PIECE, 128), BF16),
            pltpu.VMEM((4, 4, 256, 128), BF16),
            pltpu.VMEM((4, 2, 8, PIECE, 128), BF16),
            pltpu.VMEM((4, 2, 3, 2, PIECE, 128), BF16),
            pltpu.VMEM((4, 2, 4, 2, PIECE, 128), BF16),
            pltpu.VMEM((4, 2, 2, 5, PIECE, 128), BF16),
            pltpu.VMEM((4, 2, 3, PIECE, 128), BF16),
            pltpu.VMEM((4, 2, 8, PIECE, 128), BF16),
            pltpu.VMEM((4, 2, 5, PIECE, 128), BF16),
            pltpu.SemaphoreType.DMA((24,)),
            pltpu.SemaphoreType.DMA((COPIES,)),
            pltpu.SemaphoreType.DMA((COPIES,)),
        ],
        compiler_params=pltpu.CompilerParams(
            collective_id=0, has_side_effects=True, vmem_limit_bytes=56 << 20
        ),
        name="fused",
    )(q, g, o, k, v, lse, slots, live, bits)


def body(queries, keys, values, outputs, grad_out, lse, tile_slot, tile_live, tile_bits):
    oq, ok, ov = fused(
        queries[0], grad_out[0], outputs[0], keys[0], values[0], lse[0], tile_slot, tile_live, tile_bits[0, 0]
    )
    return oq[None], ok[None], ov[None]


def solution(mesh):
    in_specs = (
        P("row", "col", None),
        P("col", "row", None),
        P("col", "row", None),
        P("row", "col", None),
        P("row", "col", None),
        P("row", None, None),
        P("row", "col", None),
        P("row", "col"),
        P("row", "col", None, None, None),
    )
    out_specs = (P("row", "col", None), P("col", "row", None), P("col", "row", None))
    return jax.shard_map(body, mesh=mesh, in_specs=in_specs, out_specs=out_specs, check_vma=False)
```

time: 77.3 us -> 68.9 us (0.89)
  the two profiles are of different devices: /device:TPU:8 before, /device:TPU:1 now
where the time goes in v3:
time: 68.9 us; the launch traced here: 68.2 us
  Pallas kernels  64.1 us (93%)
  local copies, waits for them, and re-layouts  2.77 us (4%)
  between operations  1.3 us (2%)
    pallas_call x1, Pallas kernels, fused(): pl.pallas_call(fused_kernel, out_shape=[jax.ShapeDtypeStruct((PIECE, 512)...  64.1 us
    unnamed x7, local copies, waits for them, and re-layouts  2.77 us

profile of v3, /device:TPU:1, one launch (start us, length us, event | category | flops | bytes accessed | tf_op | source)
XLA Modules:
  0.0 68.2 jit_solution(18400869963956470029)
XLA Ops:
  1.3 64.1 %fused.1 = (bf16[32,512]{1,0:T(8,128)(2,1)}, bf16[32,512]{1,0:T(8,128)(2,1)}, bf16[32,512]{1,0:T(8,128)(2,1)}) custom-call(bf16[32,512]{1,0:T(8,128)(2,1)} %bitcast.11, bf16[32,512]{1,0:T(8,128)(2,1)} %bitcast.12, bf16[32,512]{1,0:T(8,128)(2,1)} %bitcast.13, bf16[32,512]{1,0:T(8,128)(2,1)} %bitcast.14, bf16[32,512]{1,0:T(8,128)(2,1)} %bitcast.15, ...), custom_call_target="tpu_custom_call" | custom-call | tf_op jit(solution)/shard_map/fused/pallas_call | solution.py:419
  65.4 0.0 copy-start.1
  65.4 1.4 %copy.16 = bf16[1,32,512]{2,1,0:T(8,128)(2,1)} copy(bf16[1,32,512]{2,1,0:T(8,128)(2,1)} %bitcast.19) | data formatting | bytes 65536
  66.8 0.0 copy-done.1
  66.8 0.0 copy-start
  66.8 0.6 copy.17
  67.4 0.2 copy-done
  67.6 0.6 copy.18
Async XLA Ops:
  65.4 1.4 %copy-start.1 = (bf16[32,512]{1,0:T(8,128)(2,1)S(1)}, bf16[32,512]{1,0:T(8,128)(2,1)}, u32[]{:S(2)}) copy-start(bf16[32,512]{1,0:T(8,128)(2,1)} %get-tuple-element.7) | copy-start | bytes 98308
  66.8 0.8 %copy-start = (bf16[32,512]{1,0:T(8,128)(2,1)S(1)}, bf16[32,512]{1,0:T(8,128)(2,1)}, u32[]{:S(2)}) copy-start(bf16[32,512]{1,0:T(8,128)(2,1)} %get-tuple-element.8) | copy-start | bytes 98308

commit v4 on v3

--- a/solution.py
+++ b/solution.py
@@ -65,7 +65,7 @@
 
 def greet(near):
     barrier = pltpu.get_barrier_semaphore()
-    for where in near.values():
+    for where in near:
         pl.semaphore_signal(barrier, inc=1, device_id=where, device_id_type=MESH)
     pl.semaphore_wait(barrier, len(near))
 
@@ -98,7 +98,7 @@
             copy.wait_send()
 
 
-OWN_TREE, MATE_TREE = CHAIN, FLAT
+OWN_TREE, MATE_TREE = CHAIN, CHAIN
 
 
 def fused_kernel(
@@ -138,7 +138,7 @@
     load("tables", [(slots_in, slots), (live_in, live), (bits_in, bits)])
     load("lse", [(lse_in, lse)])
 
-    greet(near)
+    greet([near["core"]] + [near[kind, other, far] for kind in "kq" for other, far in ((1, 0), (0, 1), (0, -1))])
     post = Post(send, recv)
 
     streams = {}
@@ -186,20 +186,10 @@
     def arrivals():
         found = []
         for n, name in enumerate(("k", "q", "v", "g")):
-            st = streams[name]
             for s in range(2):
-                first = 0.0 if s == 0 else (2.6 if st["kind"] == "k" else 3.6)
-                first += 0.4 * n + (1.5 if name == "g" else 0.0)
-                if s == 1:
-                    found.append((first, name, 1, 0))
-                for d in st["trees"][s]:
-                    when, at_d = first, d
-                    while at_d != 0:
-                        up = st["trees"][s][at_d]
-                        when += 2.9 + 0.6 * (abs(at_d - up) - 1)
-                        at_d = up
-                    found.append((when, name, s, d))
-        return sorted(found)
+                for d in ((0,) if s else ()) + tuple(streams[name]["trees"][s]):
+                    found.append((abs(d) + s, -s, n, -d, name, d))
+        return [(name, -s, d) for _, s, _, _, name, d in sorted(found)]
 
     for name in ("k", "q", "v"):
         loaded(name)
@@ -234,7 +224,7 @@
             edge = jnp.bitwise_and(jnp.right_shift(word, bit_of), 1)
             bias[pl.ds(down + r * 16, 16), pl.ds(across, 128)] = jnp.where(edge == 1, 0.0, NEG)
 
-    for _, name, s, d in arrivals():
+    for name, s, d in arrivals():
         arrive(streams[name], s, d)
     for n in ("q", "g"):
         st = streams[n]

time: 68.9 us -> 66.5 us (0.965)
  Pallas kernels: 64.1 us -> 62.1 us
    pallas_call x1, Pallas kernels: 64.1 us -> 62.1 us  [fused(): pl.pallas_call(fused_kernel, out_shape=[jax.ShapeDtypeStruct((PIECE, 512)...]
where the time goes in v4:
time: 66.5 us; the launch traced here: 66.2 us
  Pallas kernels  62.1 us (93%)
  local copies, waits for them, and re-layouts  2.77 us (4%)
  between operations  1.3 us (2%)
    pallas_call x1, Pallas kernels, fused(): pl.pallas_call(fused_kernel, out_shape=[jax.ShapeDtypeStruct((PIECE, 512)...  62.1 us
    unnamed x7, local copies, waits for them, and re-layouts  2.77 us

profile of v4, /device:TPU:1, one launch (start us, length us, event | category | flops | bytes accessed | tf_op | source)
XLA Modules:
  0.0 66.2 jit_solution(17952492857481486470)
XLA Ops:
  1.3 62.1 %fused.1 = (bf16[32,512]{1,0:T(8,128)(2,1)}, bf16[32,512]{1,0:T(8,128)(2,1)}, bf16[32,512]{1,0:T(8,128)(2,1)}) custom-call(bf16[32,512]{1,0:T(8,128)(2,1)} %bitcast.11, bf16[32,512]{1,0:T(8,128)(2,1)} %bitcast.12, bf16[32,512]{1,0:T(8,128)(2,1)} %bitcast.13, bf16[32,512]{1,0:T(8,128)(2,1)} %bitcast.14, bf16[32,512]{1,0:T(8,128)(2,1)} %bitcast.15, ...), custom_call_target="tpu_custom_call" | custom-call | tf_op jit(solution)/shard_map/fused/pallas_call | solution.py:409
  63.4 0.0 copy-start.1
  63.4 1.4 %copy.16 = bf16[1,32,512]{2,1,0:T(8,128)(2,1)} copy(bf16[1,32,512]{2,1,0:T(8,128)(2,1)} %bitcast.19) | data formatting | bytes 65536
  64.8 0.0 copy-done.1
  64.8 0.0 copy-start
  64.8 0.6 copy.17
  65.4 0.2 copy-done
  65.6 0.6 copy.18
Async XLA Ops:
  63.4 1.4 %copy-start.1 = (bf16[32,512]{1,0:T(8,128)(2,1)S(1)}, bf16[32,512]{1,0:T(8,128)(2,1)}, u32[]{:S(2)}) copy-start(bf16[32,512]{1,0:T(8,128)(2,1)} %get-tuple-element.7) | copy-start | bytes 98308
  64.8 0.8 %copy-start = (bf16[32,512]{1,0:T(8,128)(2,1)S(1)}, bf16[32,512]{1,0:T(8,128)(2,1)}, u32[]{:S(2)}) copy-start(bf16[32,512]{1,0:T(8,128)(2,1)} %get-tuple-element.8) | copy-start | bytes 98308

commit v5 on v4

--- a/solution.py
+++ b/solution.py
@@ -103,7 +103,7 @@
 
 def fused_kernel(
     q, g, o, k, v, lse_in, slots_in, live_in, bits_in,
-    oq, ok, ov,
+    result,
     qa, ga, ka, va, o_s, lse, bits, slots, live,
     bias, delta_t, qt, gt, kc, vc, kt, prob, score,
     dqp, dkv, core_land, kv_leaf, kv_mine, kv_root, q_leaf, q_mine, q_root,
@@ -111,6 +111,7 @@
 ):
     xl, z, xh, y, c = places()
     near = neighbours(xl, z, xh, y, c)
+    oq, ok, ov = result.at[0], result.at[1], result.at[2]
     rows, keys = qa.shape[1], ka.shape[1]
     scale = 0.125
 
@@ -408,9 +409,9 @@
     rows, keys = 1024, 512
     return pl.pallas_call(
         fused_kernel,
-        out_shape=[jax.ShapeDtypeStruct((PIECE, 512), BF16)] * 3,
+        out_shape=jax.ShapeDtypeStruct((3, PIECE, 512), BF16),
         in_specs=[hbm] * 9,
-        out_specs=[vmem] * 3,
+        out_specs=vmem,
         scratch_shapes=[
             pltpu.VMEM((4, rows, 128), BF16),
             pltpu.VMEM((5, rows, 128), BF16),
@@ -451,10 +452,10 @@
 
 
 def body(queries, keys, values, outputs, grad_out, lse, tile_slot, tile_live, tile_bits):
-    oq, ok, ov = fused(
+    result = fused(
         queries[0], grad_out[0], outputs[0], keys[0], values[0], lse[0], tile_slot, tile_live, tile_bits[0, 0]
     )
-    return oq[None], ok[None], ov[None]
+    return result[0:1], result[1:2], result[2:3]
 
 
 def solution(mesh):

time: 66.5 us -> 65 us (0.977)
  local copies, waits for them, and re-layouts: 2.77 us -> 1.43 us
    unnamed x7 -> x0, local copies, waits for them, and re-layouts: 2.77 us -> none
    slice x0 -> x1, local copies, waits for them, and re-layouts: none -> 1.43 us  [body(): return (result[0:1], result[1:2], result[2:3])]
where the time goes in v5:
time: 65 us; the launch traced here: 64.8 us
  Pallas kernels  62.1 us (96%)
  local copies, waits for them, and re-layouts  1.43 us (2%)
  between operations  1.29 us (2%)
    pallas_call x1, Pallas kernels, fused(): pl.pallas_call(fused_kernel, out_shape=jax.ShapeDtypeStruct((3, PIECE, 51...  62.1 us
    slice x1, local copies, waits for them, and re-layouts, body(): return (result[0:1], result[1:2], result[2:3])  1.43 us

profile of v5, /device:TPU:1, one launch (start us, length us, event | category | flops | bytes accessed | tf_op | source)
XLA Modules:
  0.0 64.8 jit_solution(932074363982893634)
XLA Ops:
  1.3 62.1 %fused.1 = bf16[3,32,512]{2,1,0:T(8,128)(2,1)} custom-call(bf16[32,512]{1,0:T(8,128)(2,1)} %bitcast.8, bf16[32,512]{1,0:T(8,128)(2,1)} %bitcast.9, bf16[32,512]{1,0:T(8,128)(2,1)} %bitcast.10, bf16[32,512]{1,0:T(8,128)(2,1)} %bitcast.11, bf16[32,512]{1,0:T(8,128)(2,1)} %bitcast.12, f32[8,1024]{1,0:T(8,128)} %bitcast.13, s32[1,1,24]{2,1,0:T(1,128)} %slots_in.1, ...), custom_call_target="tpu_custom_call" | custom-call | tf_op jit(solution)/shard_map/fused/pallas_call | solution.py:410
  63.4 1.4 %fusion = (bf16[1,32,512]{2,1,0:T(8,128)(2,1)}, bf16[1,32,512]{2,1,0:T(8,128)(2,1)}, bf16[1,32,512]{2,1,0:T(8,128)(2,1)}) fusion(bf16[3,32,512]{2,1,0:T(8,128)(2,1)} %fused.1), kind=kLoop, calls=%fused_computation | loop fusion | bytes 196608 | tf_op jit(solution)/shard_map/slice | solution.py:458
